TPU v7x, 128 devices: a whole 4x4x4 slice. The times are simulated.
128 devices in a mesh: tile: 16 (over y_lo, x, core), subap: 8 (over y_hi, z).
Axes of the slice: x: 4, y: 4 (y_hi: 2, y_lo: 2; y = y_hi * 2 + y_lo), z: 4, core: 2. Of those that a mesh axis runs over, the one named last changes fastest.
Arguments:
- pulses: bfloat16 [16, 8, 2, 128, 16384], P('tile', 'subap'), may hold values from -6 to 6
- footprint: int32 [16, 8, 32], P('tile', 'subap'), may hold values from 0 to 47, as said below
- offsets: int32 [48], replicated, may hold values from 0 to 15872
- azimuth: bfloat16 [48, 16, 8, 2, 256, 128], P('tile', None, 'subap'), may hold values from -0.09375 to 0.09375
- range_interp: bfloat16 [48, 2, 512, 256], P('tile'), may hold values from -0.1875 to 0.1875
Outputs:
- image: float32 [48, 2, 256, 256], P('tile', None, 'subap')
Inputs may be any that keep to these rules, and one draw needn't show every extreme that they name: For every o, footprint[k, s, o * 2 : (o + 1) * 2] holds 2 different tiles of o * 3 to (o + 1) * 3 - 1.
All inputs are finite; a program needn't handle non-finite values.
Results may differ from a plain program's by a relative error of at most 0.0029.
Values may be sent and summed in bfloat16 or wider, within the bound.
No kernel may reach another device: no remote copies, remote signals or barrier semaphores. Data moves between devices by JAX's collectives and lax.ppermute only.
A program may use at most 128 MiB of HBM per device.

v0:
```python
import jax
import jax.numpy as jnp
from jax import lax
from jax.sharding import PartitionSpec as P


def combine(prod):
    real = prod[..., 0, 0, :, :] - prod[..., 1, 1, :, :]
    imag = prod[..., 0, 1, :, :] + prod[..., 1, 0, :, :]
    return jnp.stack([real, imag], axis=-3)


def on_device(pulses, footprint, offsets, azimuth, range_interp):
    tiles = offsets.shape[0]
    width = range_interp.shape[2]
    block = pulses[0, 0]

    def cut(start):
        return lax.dynamic_slice_in_dim(block, start, width, 2)

    windows = jax.vmap(cut)(offsets)
    tile_ids = jnp.arange(tiles, dtype=jnp.int32)
    hit = jnp.any(footprint[0, 0][None, :] == tile_ids[:, None], axis=1).astype(jnp.bfloat16)
    windows = windows * hit[:, None, None, None]
    arrived = lax.all_to_all(windows[:, None], "tile", split_axis=0, concat_axis=1, tiled=True)
    prod = jnp.einsum(
        "tkcpr,tdru->tkcdpu", arrived, range_interp, preferred_element_type=jnp.float32
    )
    ranged = combine(prod).astype(jnp.bfloat16)
    sub_image = combine(
        jnp.einsum(
            "tkcap,tkdpu->tcdau", azimuth[:, :, 0], ranged, preferred_element_type=jnp.float32
        )
    )
    raw = lax.psum(sub_image, "subap")
    power = jnp.mean(raw * raw, axis=(1, 2, 3))
    height = raw.shape[2] // lax.axis_size("subap")
    own_rows = lax.dynamic_slice_in_dim(raw, lax.axis_index("subap") * height, height, 2)
    return own_rows / jnp.sqrt(power + 1e-06)[:, None, None, None]


def solution(mesh):
    in_specs = (
        P("tile", "subap", None, None, None),
        P("tile", "subap", None),
        P(),
        P("tile", None, "subap", None, None, None),
        P("tile", None, None, None),
    )
    out_specs = P("tile", None, "subap", None)
    return jax.shard_map(
        on_device, mesh=mesh, in_specs=in_specs, out_specs=out_specs, check_vma=False
    )
```

profile of v0, /device:TPU:0, one launch (start us, length us, event | category | flops | bytes accessed | tf_op | source)
XLA Modules:
  0.0 380.4 jit_solution(2117407463803907995)
XLA Ops:
  6.5 0.0 copy-start
  6.5 0.0 copy-start.2
  6.5 0.0 copy-start.3
  6.5 0.0 all-reduce.3.cloned.1.call-start
  6.5 21.2 %copy.46 = bf16[1,1,2,128,16384]{3,2,4,1,0:T(2,128)(2,1)} copy(bf16[1,1,2,128,16384]{4,3,2,1,0:T(8,128)(2,1)} %param.5) | data formatting | bytes 16777216 | tf_op args[0]
  27.8 0.0 copy-done.2
  27.8 0.0 copy-done.3
  27.8 0.1 fusion.21
  27.9 30.5 %gather_fusion = bf16[48,2,128,512]{2,1,3,0:T(2,128)(2,1)} fusion(bf16[2,128,16384]{1,0,2:T(2,128)(2,1)} %bitcast.66, s32[48]{0:T(128)S(1)} %fusion.23), kind=kCustom, calls=%fused_computation | custom fusion | bytes 25166400 | tf_op jit(solution)/shard_map/vmap()/gather | solution.py:19
  58.4 13.9 %fusion.2 = bf16[48,1,2,128,512]{3,2,4,1,0:T(2,128)(2,1)S(1)} fusion(bf16[48,2,128,512]{2,1,3,0:T(2,128)(2,1)} %gather_fusion, bf16[48]{0:T(256)(128)(2,1)S(1)} %convert_element_type.8), kind=kLoop, calls=%fused_computation.4 | loop fusion | flops 6291456 | bytes 25165920 | tf_op jit(solution)/shard_map/mul | solution.py:24
  72.3 145.5 %all_to_all.18 = bf16[48,1,2,128,512]{3,2,4,1,0:T(2,128)(2,1)} all-to-all(bf16[48,1,2,128,512]{3,2,4,1,0:T(2,128)(2,1)S(1)} %fusion.2), channel_id=1, replica_groups=mesh['tile'=16,'subap'=8] {'tile'}, dimensions={0} | all-to-all | bytes 25165824 | tf_op jit(solution)/shard_map/all_to_all | solution.py:25
  217.8 30.9 %copy.49 = bf16[16,3,1,2,128,512]{5,4,3,0,1,2:T(8,128)(2,1)} copy(bf16[16,3,1,2,128,512]{4,3,5,1,0,2:T(2,128)(2,1)} %bitcast.67) | data formatting | bytes 25165824 | tf_op jit(solution)/shard_map/all_to_all | solution.py:25
  248.7 0.0 copy-done
  248.7 14.4 %fusion.3 = f32[3,16,2,2,128,256]{5,4,3,2,1,0:T(8,128)} fusion(bf16[16,3,1,2,128,512]{5,4,3,0,1,2:T(8,128)(2,1)} %copy.49, bf16[3,2,512,256]{3,2,1,0:T(8,128)(2,1)S(1)} %copy-done), kind=kOutput, calls=%fused_computation.5 | convolution fusion | flops 6442450944 | bytes 39321600 | tf_op jit(solution)/shard_map/tkcpr,tdru->tkcdpu/dot_general | solution.py:26
  263.2 0.0 slice-start
  263.2 6.0 %fusion.13 = bf16[3,16,1,128,256]{4,3,1,0,2:T(8,128)(2,1)S(1)} fusion(f32[3,16,2,2,128,256]{5,4,3,2,1,0:T(8,128)} %fusion.3), kind=kLoop, calls=%fused_computation.17 | loop fusion | flops 3145728 | bytes 15728640 | tf_op jit(solution)/shard_map/sub | solution.py:8
  269.2 0.0 slice-start.1
  269.2 5.8 %fusion.14 = bf16[3,16,1,128,256]{4,3,1,0,2:T(8,128)(2,1)S(1)} fusion(f32[3,16,2,2,128,256]{5,4,3,2,1,0:T(8,128)} %fusion.3), kind=kLoop, calls=%fused_computation.18 | loop fusion | flops 3145728 | bytes 15728640 | tf_op jit(solution)/shard_map/add | solution.py:9
  275.0 0.0 slice-done
  275.0 0.0 slice-done.1
  275.0 0.0 copy-start.1
  275.0 3.4 fusion.15
  278.4 0.2 fusion.20
  278.7 1.3 pad_maximum_fusion
  279.9 0.0 all-reduce.3.cloned.1.call-update
  279.9 90.3 %all-reduce.3.cloned.1.call-done = f32[3,2,256,256]{3,2,1,0:T(8,128)} async-done(((f32[3,2,256,256]{3,2,1,0:T(8,128)}), f32[3,2,256,256]{3,2,1,0:T(8,128)}) %all-reduce.3.cloned.1.call-update) | async-done | bytes 1572880 | tf_op jit(solution)/shard_map/psum | solution.py:35
  370.2 1.7 multiply_reduce_fusion
  371.9 1.7 dynamic-slice_divide_fusion
  373.6 0.0 copy-done.1
  (4 shorter events, 0.0 us)
Async XLA Ops:
  6.5 242.2 %copy-start = (bf16[3,2,512,256]{3,2,1,0:T(8,128)(2,1)S(1)}, bf16[3,2,512,256]{3,2,1,0:T(8,128)(2,1)}, u32[]{:S(2)}) copy-start(bf16[3,2,512,256]{3,2,1,0:T(8,128)(2,1)} %param.9) | copy-start | bytes 4718596
  6.5 21.2 %copy-start.2 = (s32[48]{0:T(128)S(1)}, s32[48]{0:T(128)}, u32[]{:S(2)}) copy-start(s32[48]{0:T(128)} %param.7) | copy-start | bytes 580
  6.5 21.3 %copy-start.3 = (s32[1,1,32]{2,1,0:T(1,128)S(1)}, s32[1,1,32]{2,1,0:T(1,128)}, u32[]{:S(2)}) copy-start(s32[1,1,32]{2,1,0:T(1,128)} %param.6) | copy-start | bytes 388
  6.5 363.7 %all-reduce.3.cloned.1.call-start = ((), (), s32[]{:S(2)}) async-start(), calls=%async_computation.1 | async-start | bytes 3145728 | tf_op jit(solution)/shard_map/psum | solution.py:35
  263.2 11.8 %slice-start = ((s8[6291456]{0:T(1024)(128)(4,1)}), s8[4194304]{0:T(1024)(128)(4,1)S(1)}, s32[]{:S(2)}) async-start(s8[6291456]{0:T(1024)(128)(4,1)} %bitcast.68), calls=%async_computation.2 | async-start | bytes 8388608
  269.2 5.8 %slice-start.1 = ((s8[6291456]{0:T(1024)(128)(4,1)}), s8[2097152]{0:T(1024)(128)(4,1)S(1)}, s32[]{:S(2)}) async-start(s8[6291456]{0:T(1024)(128)(4,1)} %bitcast.68), calls=%async_computation.3 | async-start | bytes 4194304
  275.0 98.6 %copy-start.1 = (bf16[3,2,512,256]{3,2,1,0:T(8,128)(2,1)S(1)}, bf16[3,2,512,256]{3,2,1,0:T(8,128)(2,1)}, u32[]{:S(2)}) copy-start(bf16[3,2,512,256]{3,2,1,0:T(8,128)(2,1)} %param.9) | copy-start | bytes 4718596
Sparse Core Ops, SparseCore 0:
  280.1 90.1 all-reduce.2
where the time goes:
time: 382 us; the launch traced here: 380 us
  blocking collectives  145 us (38%)
  waiting for transfers between devices  90.3 us (24%)
  local copies, waits for them, and re-layouts  82.7 us (22%)
  other arithmetic  30.7 us (8%)
  matrix products  17.8 us (5%)
  between operations  13.5 us (4%)
    all_to_all x1, blocking collectives, on_device(): lax.all_to_all(windows[:, None], 'tile', split_axis=0, concat_axis=1, til...  145 us
    psum x1, waiting for transfers between devices, on_device(): raw = lax.psum(sub_image, 'subap')  90.3 us
    all_to_all x1, local copies, waits for them, and re-layouts, on_device(): lax.all_to_all(windows[:, None], 'tile', split_axis=0, concat_axis=1, til...  30.9 us
    gather x1, local copies, waits for them, and re-layouts, cut(): return lax.dynamic_slice_in_dim(block, start, width, 2)  30.5 us
    unnamed x13, local copies, waits for them, and re-layouts  21.3 us
    dot_general x1, matrix products, on_device(): jnp.einsum('tkcpr,tdru->tkcdpu', arrived, range_interp, preferred_element...  14.4 us
    mul x1, other arithmetic, on_device(): windows = windows * hit[:, None, None, None]  13.9 us
  transfers between devices with their start and end apart: 1, of which 1 were waited for; matrix products, arithmetic and copies ran while one was open for 0% of the time, Pallas kernels for 0%

commit v1 on v0

--- a/solution.py
+++ b/solution.py
@@ -32,7 +32,7 @@
             "tkcap,tkdpu->tcdau", azimuth[:, :, 0], ranged, preferred_element_type=jnp.float32
         )
     )
-    raw = lax.psum(sub_image, "subap")
+    raw = jnp.sum(lax.all_gather(sub_image, "subap"), axis=0)
     power = jnp.mean(raw * raw, axis=(1, 2, 3))
     height = raw.shape[2] // lax.axis_size("subap")
     own_rows = lax.dynamic_slice_in_dim(raw, lax.axis_index("subap") * height, height, 2)

time: 382 us -> 449 us (1.18)
  waiting for transfers between devices: 90.3 us -> 145 us
  other arithmetic: 30.7 us -> 35.7 us
  matrix products: 17.8 us -> 22.4 us
    all_gather x0 -> x1, waiting for transfers between devices: none -> 145 us  [on_device(): raw = jnp.sum(lax.all_gather(sub_image, 'subap'), axis=0)]
    psum x1 -> x0, waiting for transfers between devices: 90.3 us -> none  [on_device(): raw = lax.psum(sub_image, 'subap')]
    reduce_sum x0 -> x1, other arithmetic: none -> 5.71 us  [on_device(): raw = jnp.sum(lax.all_gather(sub_image, 'subap'), axis=0)]
    unnamed x13 -> x10, local copies, waits for them, and re-layouts: 21.3 us -> 22.6 us
where the time goes in v1:
time: 449 us; the launch traced here: 447 us
  blocking collectives  145 us (32%)
  waiting for transfers between devices  145 us (32%)
  local copies, waits for them, and re-layouts  85.1 us (19%)
  other arithmetic  35.7 us (8%)
  matrix products  22.4 us (5%)
  between operations  13.5 us (3%)
    all_to_all x1, blocking collectives, on_device(): lax.all_to_all(windows[:, None], 'tile', split_axis=0, concat_axis=1, til...  145 us
    all_gather x1, waiting for transfers between devices, on_device(): raw = jnp.sum(lax.all_gather(sub_image, 'subap'), axis=0)  145 us
    all_to_all x1, local copies, waits for them, and re-layouts, on_device(): lax.all_to_all(windows[:, None], 'tile', split_axis=0, concat_axis=1, til...  30.9 us
    gather x1, local copies, waits for them, and re-layouts, cut(): return lax.dynamic_slice_in_dim(block, start, width, 2)  30.5 us
    unnamed x10, local copies, waits for them, and re-layouts  22.6 us
    dot_general x1, matrix products, on_device(): jnp.einsum('tkcpr,tdru->tkcdpu', arrived, range_interp, preferred_element...  14.5 us
    mul x1, other arithmetic, on_device(): windows = windows * hit[:, None, None, None]  13.9 us
  transfers between devices with their start and end apart: 1, of which 1 were waited for; matrix products, arithmetic and copies ran while one was open for 0% of the time, Pallas kernels for 0%

profile of v1, /device:TPU:0, one launch (start us, length us, event | category | flops | bytes accessed | tf_op | source)
XLA Modules:
  0.0 447.0 jit_solution(7409409024850660174)
XLA Ops:
  6.5 0.0 copy-start
  6.5 0.0 copy-start.2
  6.5 0.0 copy-start.3
  6.5 0.0 all-gather.3.cloned.1.call-start
  6.5 21.2 %copy.44 = bf16[1,1,2,128,16384]{3,2,4,1,0:T(2,128)(2,1)} copy(bf16[1,1,2,128,16384]{4,3,2,1,0:T(8,128)(2,1)} %param.5) | data formatting | bytes 16777216 | tf_op args[0]
  27.8 0.0 copy-done.2
  27.8 0.0 copy-done.3
  27.8 0.1 fusion.23
  27.9 30.5 %gather_fusion = bf16[48,2,128,512]{2,1,3,0:T(2,128)(2,1)} fusion(bf16[2,128,16384]{1,0,2:T(2,128)(2,1)} %bitcast.75, s32[48]{0:T(128)S(1)} %fusion.25), kind=kCustom, calls=%fused_computation | custom fusion | bytes 25166400 | tf_op jit(solution)/shard_map/vmap()/gather | solution.py:19
  58.4 13.9 %fusion.2 = bf16[48,1,2,128,512]{3,2,4,1,0:T(2,128)(2,1)S(1)} fusion(bf16[48,2,128,512]{2,1,3,0:T(2,128)(2,1)} %gather_fusion, bf16[48]{0:T(256)(128)(2,1)S(1)} %convert_element_type.8), kind=kLoop, calls=%fused_computation.4 | loop fusion | flops 6291456 | bytes 25165920 | tf_op jit(solution)/shard_map/mul | solution.py:24
  72.3 145.5 %all_to_all.18 = bf16[48,1,2,128,512]{3,2,4,1,0:T(2,128)(2,1)} all-to-all(bf16[48,1,2,128,512]{3,2,4,1,0:T(2,128)(2,1)S(1)} %fusion.2), channel_id=1, replica_groups=mesh['tile'=16,'subap'=8] {'tile'}, dimensions={0} | all-to-all | bytes 25165824 | tf_op jit(solution)/shard_map/all_to_all | solution.py:25
  217.8 30.9 %copy.47 = bf16[16,3,1,2,128,512]{5,4,3,0,1,2:T(8,128)(2,1)} copy(bf16[16,3,1,2,128,512]{4,3,5,1,0,2:T(2,128)(2,1)} %bitcast.76) | data formatting | bytes 25165824 | tf_op jit(solution)/shard_map/all_to_all | solution.py:25
  248.6 0.0 copy-done
  248.6 14.5 %fusion.3 = f32[3,16,2,2,128,256]{5,4,3,2,1,0:T(8,128)} fusion(bf16[16,3,1,2,128,512]{5,4,3,0,1,2:T(8,128)(2,1)} %copy.47, bf16[3,2,512,256]{3,2,1,0:T(8,128)(2,1)S(1)} %copy-done), kind=kOutput, calls=%fused_computation.5 | convolution fusion | flops 6442450944 | bytes 39321600 | tf_op jit(solution)/shard_map/tkcpr,tdru->tkcdpu/dot_general | solution.py:26
  263.2 5.9 %fusion.12 = bf16[3,16,1,128,256]{4,3,1,0,2:T(8,128)(2,1)S(1)} fusion(f32[3,16,2,2,128,256]{5,4,3,2,1,0:T(8,128)} %fusion.3), kind=kLoop, calls=%fused_computation.16 | loop fusion | flops 3145728 | bytes 15728640 | tf_op jit(solution)/shard_map/sub | solution.py:8
  269.1 7.4 %fusion.13 = bf16[3,16,1,128,256]{4,3,1,0,2:T(8,128)(2,1)} fusion(f32[3,16,2,2,128,256]{5,4,3,2,1,0:T(8,128)} %fusion.3), kind=kLoop, calls=%fused_computation.17 | loop fusion | flops 3145728 | bytes 15728640 | tf_op jit(solution)/shard_map/add | solution.py:9
  276.5 7.8 %fusion.14 = f32[3,2,2,256,256]{3,4,1,2,0:T(8,128)S(1)} fusion(bf16[3,16,1,128,256]{4,3,1,0,2:T(8,128)(2,1)} %fusion.13, bf16[3,16,1,128,256]{4,3,1,0,2:T(8,128)(2,1)S(1)} %fusion.12, bf16[3,16,1,2,256,128]{5,4,3,2,1,0:T(8,128)(2,1)} %param.8), kind=kOutput, calls=%fused_computation.18 | convolution fusion | flops 3224371200 | bytes 15728640 | tf_op jit(solution)/shard_map/tkcap,tkdpu->tcdau/dot_general | solution.py:31
  284.3 0.1 fusion.20
  284.4 0.1 fusion.22
  284.5 1.4 pad_maximum_fusion
  285.9 0.0 all-gather.3.cloned.1.call-update
  286.0 144.9 %all-gather.3.cloned.1.call-done = f32[24,2,256,256]{2,3,0,1:T(8,128)} async-done(((f32[3,2,256,256]{2,3,0,1:T(8,128)}), f32[24,2,256,256]{2,3,0,1:T(8,128)}) %all-gather.3.cloned.1.call-update) | async-done | bytes 12582928 | tf_op jit(solution)/shard_map/all_gather | solution.py:35
  430.9 0.0 copy-start.1
  430.9 5.7 %reduce_sum.18 = f32[3,2,256,256]{2,3,0,1:T(8,128)S(1)} reduce(f32[8,3,2,256,256]{3,4,1,0,2:T(8,128)} %bitcast.77, f32[]{:T(128)} %constant.2.clone.1), dimensions={0}, to_apply=%region_1.0 | reduce | flops 2752512 | bytes 14155780 | tf_op jit(solution)/shard_map/reduce_sum | solution.py:35
  436.6 0.3 multiply_reduce_fusion
  436.8 1.1 constant_dynamic-slice_fusion
  438.0 1.4 copy.70
  439.4 0.8 broadcast_divide_fusion
  440.1 0.0 copy-done.1
  (3 shorter events, 0.0 us)
Async XLA Ops:
  6.5 242.1 %copy-start = (bf16[3,2,512,256]{3,2,1,0:T(8,128)(2,1)S(1)}, bf16[3,2,512,256]{3,2,1,0:T(8,128)(2,1)}, u32[]{:S(2)}) copy-start(bf16[3,2,512,256]{3,2,1,0:T(8,128)(2,1)} %param.9) | copy-start | bytes 4718596
  6.5 21.2 %copy-start.2 = (s32[48]{0:T(128)S(1)}, s32[48]{0:T(128)}, u32[]{:S(2)}) copy-start(s32[48]{0:T(128)} %param.7) | copy-start | bytes 580
  6.5 21.3 %copy-start.3 = (s32[1,1,32]{2,1,0:T(1,128)S(1)}, s32[1,1,32]{2,1,0:T(1,128)}, u32[]{:S(2)}) copy-start(s32[1,1,32]{2,1,0:T(1,128)} %param.6) | copy-start | bytes 388
  6.5 424.3 %all-gather.3.cloned.1.call-start = ((), (), s32[]{:S(2)}) async-start(), calls=%async_computation.1 | async-start | bytes 14155776 | tf_op jit(solution)/shard_map/all_gather | solution.py:35
  430.9 9.3 %copy-start.1 = (bf16[3,2,512,256]{3,2,1,0:T(8,128)(2,1)S(1)}, bf16[3,2,512,256]{3,2,1,0:T(8,128)(2,1)}, u32[]{:S(2)}) copy-start(bf16[3,2,512,256]{3,2,1,0:T(8,128)(2,1)} %param.9) | copy-start | bytes 4718596
Sparse Core Ops, SparseCore 0:
  286.1 144.7 all-gather.2
